TPU v7x, 32 devices: a whole 2x2x4 slice. The times are simulated.
32 devices in a mesh: groups: 2 (over y), dp: 4 (over z), seq: 4 (over x, core).
Axes of the slice: x: 2, y: 2, z: 4, core: 2. Of those that a mesh axis runs over, the one named last changes fastest.
Arguments:
- query_rows: bfloat16 [8, 1024, 8192], P(('groups', 'dp'), 'seq'), parts along dimension 0, may hold values from -60 to 60
- key_rows: bfloat16 [8, 1024, 1024], P(('groups', 'dp'), 'seq'), parts along dimension 0, may hold values from -4 to 4
- placed_value_rows: bfloat16 [8, 1024, 1024], P(('groups', 'dp'), 'seq'), parts along dimension 0, may hold values from -4 to 4
- doc_lengths: int32 [8, 8], P(('groups', 'dp')), parts along dimension 0, may hold values from 1 to 512, 1024 in all within a row
- span_order: int32 [8, 8], P(('groups', 'dp')), parts along dimension 0, may hold values from 0 to 7, each once within a row
- out_weight: bfloat16 [8192, 8192], P('dp', 'seq'), may hold values from -0.25 to 0.25
Outputs:
- whitened: float32 [32, 512, 8192], P(('groups', 'seq'), None, 'dp'), parts along dimension 0
There are 2 independent parts, one for each index of `groups`. A program takes and returns all parts, laid end to end along the dimension named above; an argument that names none is the same for every part. Nothing has to cross between parts.
All inputs are finite; a program needn't handle non-finite values.
Results may differ from a plain program's by a relative error of at most 0.00073.
Values may be sent and summed in bfloat16 or wider, within the bound.
A program may use at most 128 MiB of HBM per device.

v0:
```python
import jax
import jax.numpy as jnp
from jax import lax
from jax.sharding import PartitionSpec as P

QUERY_HEADS = 64
KEY_VALUE_HEADS = 8
HEAD_SIZE = 128
BLOCK_W = 512
NB = 16


def doc_numbers(positions, lengths):
    starts = jnp.cumsum(lengths) - lengths
    return jnp.sum((positions[:, None] >= starts[None, :]).astype(jnp.int32), axis=1)


def local_attention(query_local, key_all, value_all, visible):
    tok_count = query_local.shape[0]
    head_group = QUERY_HEADS // KEY_VALUE_HEADS
    results = []
    for kv_index in range(KEY_VALUE_HEADS):
        key_head = key_all[:, kv_index * HEAD_SIZE : (kv_index + 1) * HEAD_SIZE]
        value_head = value_all[:, kv_index * HEAD_SIZE : (kv_index + 1) * HEAD_SIZE]
        query_group = query_local[
            :, kv_index * head_group * HEAD_SIZE : (kv_index + 1) * head_group * HEAD_SIZE
        ].reshape(tok_count, head_group, HEAD_SIZE)
        scores = jnp.einsum(
            "qgd,kd->gqk", query_group, key_head, preferred_element_type=jnp.float32
        ) * HEAD_SIZE ** (-0.5)
        scores = jnp.where(visible[None], scores, -1e30)
        largest = jnp.max(scores, axis=2, keepdims=True)
        lifted = jnp.exp(scores - largest)
        weights = (lifted / jnp.sum(lifted, axis=2, keepdims=True)).astype(jnp.bfloat16)
        mixed = jnp.einsum("gqk,kd->qgd", weights, value_head, preferred_element_type=jnp.float32)
        results.append(mixed.reshape(tok_count, head_group * HEAD_SIZE))
    return jnp.concatenate(results, axis=1)


def block_outer(blocks):
    return jnp.einsum("rbi,rbj->bij", blocks, blocks, precision=lax.Precision.HIGHEST)


def shards(query_rows, key_rows, placed_value_rows, doc_lengths, span_order, out_weight):
    tok_count = query_rows.shape[1]
    seq_count = lax.axis_size("seq")
    seq_length = tok_count * seq_count
    span_rows = tok_count // 2
    lengths = doc_lengths[0]
    placement = span_order[0]
    query_local = query_rows[0]
    key_local = key_rows[0]
    value_local = placed_value_rows[0]
    key_all, value_all = (
        lax.all_gather(key_local, "seq", axis=0, tiled=True),
        lax.all_gather(value_local, "seq", axis=0, tiled=True),
    )
    row_ids = jnp.arange(seq_length, dtype=jnp.int32)
    positions = placement[row_ids // span_rows] * span_rows + row_ids % span_rows
    doc_ids = doc_numbers(positions, lengths)
    own_start = lax.axis_index("seq") * tok_count
    query_pos = lax.dynamic_slice_in_dim(positions, own_start, tok_count, 0)
    query_docs = lax.dynamic_slice_in_dim(doc_ids, own_start, tok_count, 0)
    visible = (query_docs[:, None] == doc_ids[None, :]) & (positions[None, :] <= query_pos[:, None])
    outputs = local_attention(query_local, key_all, value_all, visible)
    blocks = outputs.reshape(tok_count, NB, BLOCK_W)
    grams = lax.psum_scatter(block_outer(blocks), "seq", scatter_dimension=0, tiled=True)
    block_count = grams.shape[0]
    traces = jnp.trace(grams, axis1=1, axis2=2)
    identity = jnp.eye(BLOCK_W, dtype=jnp.float32)
    damped = grams + (0.1 * traces / BLOCK_W)[:, None, None] * identity
    summed = lax.psum(damped, "dp")
    upper = jnp.swapaxes(jnp.linalg.cholesky(summed), 1, 2)
    weight_blocks = out_weight.astype(jnp.float32).reshape(
        out_weight.shape[0], block_count, BLOCK_W
    )
    return jnp.einsum("bij,obj->bio", upper, weight_blocks, precision=lax.Precision.HIGHEST)


def solution(mesh):
    in_specs = (
        P(("groups", "dp"), "seq", None),
        P(("groups", "dp"), "seq", None),
        P(("groups", "dp"), "seq", None),
        P(("groups", "dp"), None),
        P(("groups", "dp"), None),
        P("dp", "seq"),
    )
    out_specs = P(("groups", "seq"), None, "dp")
    return jax.shard_map(shards, mesh=mesh, in_specs=in_specs, out_specs=out_specs, check_vma=False)
```

profile of v0, /device:TPU:0, one launch (start us, length us, event | category | flops | bytes accessed | tf_op | source)
XLA Modules:
  0.0 871.0 jit_solution(3621411485237233564)
XLA Ops:
  11.9 4.4 compare_select_fusion.1
  17.9 6.4 copy.92
  28.6 5.6 all-gather.5.cloned.1.call-done
  34.2 7.1 fusion.119
  41.3 17.3 %all-gather.7.cloned.1.call-done = bf16[1,1024,1024]{1,2,0:T(8,128)(2,1)} async-done(((bf16[1,256,1024]{1,2,0:T(8,128)(2,1)}), bf16[1,1024,1024]{1,2,0:T(8,128)(2,1)}) %all-gather.7.cloned.1.call-update) | async-done | bytes 2097168 | tf_op jit(solution)/shard_map/all_gather | solution.py:56
  63.1 7.1 fusion.118
  70.3 4.2 fusion.46
  75.9 7.3 fusion.120
  87.8 20.6 %fusion.121 = (f32[8,256]{1,0:T(8,128)S(1)}, f32[8,256,1024]{1,2,0:T(8,128)}) fusion(pred[256,1024]{0,1:T(8,128)(4,1)S(1)} %compare_and_fusion, bf16[256,8,128]{0,2,1:T(8,128)(2,1)} %bitcast.316, bf16[1024,1024]{1,0:T(8,128)(2,1)} %bitcast.324), kind=kOutput, calls=%fused_computation.208 | convolution fusion | flops 545260544 | bytes 9445376 | tf_op jit(solution)/shard_map/sub | solution.py:33
  108.4 5.3 fusion.49
  115.2 7.3 fusion.122
  122.5 5.2 fusion.50
  130.3 7.3 fusion.123
  137.7 5.2 fusion.51
  145.4 7.3 fusion.124
  152.7 5.2 fusion.52
  160.4 7.3 fusion.125
  167.8 5.2 fusion.53
  184.2 35.3 %fusion.126 = f32[16,512,512]{1,2,0:T(8,128)} fusion(f32[256,16,512]{2,0,1:T(8,128)} %constant_dynamic-update-slice_fusion), kind=kOutput, calls=%fused_computation.213 | convolution fusion | flops 12884901888 | bytes 25165824 | tf_op jit(solution)/shard_map/rbi,rbj->bij/dot_general | solution.py:41
  219.8 124.9 %reduce-scatter.2.cloned.1.call-done = f32[4,512,512]{1,2,0:T(8,128)} async-done(((f32[16,512,512]{1,2,0:T(8,128)}), f32[4,512,512]{1,2,0:T(8,128)}) %reduce-scatter.2.cloned.1.call-update) | async-done | bytes 4194320 | tf_op jit(solution)/shard_map/reduce_scatter | solution.py:67
  347.7 4.9 multiply_add_fusion
  352.8 155.0 %all-reduce.3.cloned.1.call-done = f32[4,512,512]{1,2,0:T(8,128)} async-done(((f32[4,512,512]{1,2,0:T(8,128)}), f32[4,512,512]{1,2,0:T(8,128)}) %all-reduce.3.cloned.1.call-update) | async-done | bytes 4194320 | tf_op jit(solution)/shard_map/psum | solution.py:72
  507.8 5.2 copy.120
  513.0 4.5 fusion.19
  519.6 46.9 %custom-call.31 = f32[4,128,128]{2,1,0:T(8,128)S(1)} custom-call(f32[4,128,128]{2,1,0:T(8,128)S(1)} %cholesky.271), custom_call_target="Cholesky" | custom-call | tf_op jit(solution)/shard_map/jit(cholesky)/cholesky | solution.py:73
  566.5 39.3 %custom-call.32 = f32[4,1,128,128]{2,3,1,0:T(8,128)S(1)} custom-call(f32[4,1,128,128]{3,2,1,0:T(8,128)S(1)} %select_bitcast_fusion.2), custom_call_target="InvertDiagBlocksLowerTriangular" | custom-call | tf_op jit(solution)/shard_map/jit(cholesky)/cholesky | solution.py:73
  610.2 47.1 %custom-call.33 = f32[4,128,128]{2,1,0:T(8,128)S(1)} custom-call(f32[4,128,128]{2,1,0:T(8,128)S(1)} %cholesky.275), custom_call_target="Cholesky" | custom-call | tf_op jit(solution)/shard_map/jit(cholesky)/cholesky | solution.py:73
  657.5 39.3 %custom-call.34 = f32[4,1,128,128]{2,3,1,0:T(8,128)S(1)} custom-call(f32[4,1,128,128]{3,2,1,0:T(8,128)S(1)} %select_bitcast_fusion.1), custom_call_target="InvertDiagBlocksLowerTriangular" | custom-call | tf_op jit(solution)/shard_map/jit(cholesky)/cholesky | solution.py:73
  703.1 47.3 %custom-call.35 = f32[4,128,128]{2,1,0:T(8,128)S(1)} custom-call(f32[4,128,128]{2,1,0:T(8,128)S(1)} %cholesky.280), custom_call_target="Cholesky" | custom-call | tf_op jit(solution)/shard_map/jit(cholesky)/cholesky | solution.py:73
  751.3 39.3 %custom-call.36 = f32[4,1,128,128]{2,3,1,0:T(8,128)S(1)} custom-call(f32[4,1,128,128]{3,2,1,0:T(8,128)S(1)} %select_bitcast_fusion), custom_call_target="InvertDiagBlocksLowerTriangular" | custom-call | tf_op jit(solution)/shard_map/jit(cholesky)/cholesky | solution.py:73
  795.0 47.1 %custom-call.37 = f32[4,128,128]{2,1,0:T(8,128)S(1)} custom-call(f32[4,128,128]{2,1,0:T(8,128)S(1)} %convolution_subtract_fusion.2), custom_call_target="Cholesky" | custom-call | tf_op jit(solution)/shard_map/jit(cholesky)/cholesky | solution.py:73
  843.3 21.0 %fusion.8 = f32[4,512,2048]{2,1,0:T(8,128)} fusion(bf16[256,4,8,512]{3,2,1,0:T(8,128)(2,1)} %bitcast.302, f32[4,512,512]{1,2,0:T(8,128)} %constant_dynamic-update-slice_fusion.8, pred[4]{0:T(512)(128)(4,1)S(1)} %or_or_fusion, pred[512,512]{0,1:T(8,128)(4,1)S(1)} %iota_compare_fusion.1), kind=kOutput, calls=%fused_computation.8 | convolution fusion | flops 25771900928 | bytes 29622276 | tf_op jit(solution)/shard_map/bij,obj->bio/dot_general | solution.py:77
  (80 shorter events, 64.7 us)
Async XLA Ops:
  6.5 27.7 %all-gather.5.cloned.1.call-start = ((), (), s32[]{:S(2)}) async-start(), calls=%async_computation.3 | async-start | bytes 2621440 | tf_op jit(solution)/shard_map/all_gather | solution.py:55
  7.3 51.3 %all-gather.7.cloned.1.call-start = ((), (), s32[]{:S(2)}) async-start(), calls=%async_computation.4 | async-start | bytes 2621440 | tf_op jit(solution)/shard_map/all_gather | solution.py:56
  9.4 335.4 %reduce-scatter.2.cloned.1.call-start = ((), (), s32[]{:S(2)}) async-start(), calls=%async_computation.1 | async-start | bytes 20971520 | tf_op jit(solution)/shard_map/reduce_scatter | solution.py:67
  175.5 5.5 copy-start.2
  175.5 6.6 copy-start.3
  175.5 7.6 copy-start.4
  219.5 288.3 %all-reduce.3.cloned.1.call-start = ((), (), s32[]{:S(2)}) async-start(), calls=%async_computation.2 | async-start | bytes 8388608 | tf_op jit(solution)/shard_map/psum | solution.py:72
  517.5 2.0 copy-start.1
  698.2 1.9 copy-start
Sparse Core Ops, SparseCore 0:
  8.9 25.2 all-gather.4
  35.8 22.8 all-gather.6
  219.7 125.0 reduce-scatter.1
  352.8 154.9 all-reduce.2
where the time goes:
time: 881 us; the launch traced here: 871 us
  other arithmetic  326 us (37%)
  waiting for transfers between devices  304 us (35%)
  matrix products  178 us (20%)
  local copies, waits for them, and re-layouts  48.8 us (6%)
  between operations  13.7 us (2%)
    another operation x16, other arithmetic, shards(): upper = jnp.swapaxes(jnp.linalg.cholesky(summed), 1, 2)  307 us
    psum x1, waiting for transfers between devices, shards(): summed = lax.psum(damped, 'dp')  155 us
    reduce_scatter x1, waiting for transfers between devices, shards(): lax.psum_scatter(block_outer(blocks), 'seq', scatter_dimension=0, tiled=T...  125 us
    sub x8, matrix products, local_attention(): lifted = jnp.exp(scores - largest)  71.5 us
    dot_general x8, matrix products, local_attention(): jnp.einsum('gqk,kd->qgd', weights, value_head, preferred_element_type=jnp...  38.6 us
    dot_general x1, matrix products, block_outer(): jnp.einsum('rbi,rbj->bij', blocks, blocks, precision=lax.Precision.HIGHEST)  35.3 us
    unnamed x19, local copies, waits for them, and re-layouts  21.1 us
    dot_general x1, matrix products, shards(): jnp.einsum('bij,obj->bio', upper, weight_blocks, precision=lax.Precision....  21 us
  transfers between devices with their start and end apart: 4, of which 4 were waited for; matrix products, arithmetic and copies ran while one was open for 3% of the time, Pallas kernels for 0%

commit v1 on v0

v1 whole, which is shorter than its diff:
```python
import functools

import jax
import jax.numpy as jnp
from jax import lax
from jax.experimental import pallas as pl
from jax.experimental.pallas import tpu as pltpu
from jax.sharding import PartitionSpec as P

QUERY_HEADS = 64
KEY_VALUE_HEADS = 8
HEAD_SIZE = 128
BLOCK_W = 512
NB = 16
TILE = 128
TILES = BLOCK_W // TILE
OFFSETS = [sum(TILES - t for t in range(i)) * TILE for i in range(TILES + 1)]
PACKED = OFFSETS[TILES]
F32 = jnp.float32
BF16 = jnp.bfloat16


def widths(count):
    out, step = [], 1
    while len(out) == 0 or out[-1] < count:
        out.append(min(count, (out[-1] if out else 0) + step))
        if len(out) >= 8:
            step = 4
    return out


def attention_kernel(span, spans, blocks, lengths_ref, order_ref, q_ref, k_ref, v_ref, gram_ref,
                     k_pos, v_pos, hi_ref, lo_ref):
    b = pl.program_id(0)
    heads = BLOCK_W // HEAD_SIZE

    @pl.when(b % (QUERY_HEADS // KEY_VALUE_HEADS // heads) == 0)
    def _():
        for r in range(spans):
            at = pl.multiple_of(order_ref[0, r] * span, span)
            k_pos[pl.ds(at, span), :] = k_ref[r * span:(r + 1) * span, :]
            v_pos[pl.ds(at, span), :] = v_ref[r * span:(r + 1) * span, :]

    def one_span(r, carry):
        place = order_ref[0, r]
        base = place * span
        pos = base + lax.broadcasted_iota(jnp.int32, (span, 1), 0)
        start = jnp.zeros((span, 1), jnp.int32)
        first = jnp.int32(0)
        total = jnp.int32(0)
        for d in range(lengths_ref.shape[1]):
            start = jnp.where(pos >= total, total, start)
            first = jnp.where(base >= total, total, first)
            total = total + lengths_ref[0, d]
        low = first // span
        needed = place - low + 1
        row = pl.multiple_of(r * span, span)

        def attend(count):
            begin = jnp.minimum(low, spans - count)
            at = pl.multiple_of(begin * span, span)
            keys = k_pos[pl.ds(at, count * span), :]
            values = v_pos[pl.ds(at, count * span), :]
            key_pos = begin * span + lax.broadcasted_iota(jnp.int32, (span, count * span), 1)
            visible = (key_pos >= start) & (key_pos <= pos)
            for h in range(heads):
                query = q_ref[pl.ds(row, span), h * HEAD_SIZE:(h + 1) * HEAD_SIZE]
                scores = lax.dot_general(query, keys, (((1,), (1,)), ((), ())),
                                         preferred_element_type=F32) * HEAD_SIZE ** (-0.5)
                scores = jnp.where(visible, scores, -1e30)
                lifted = jnp.exp(scores - jnp.max(scores, axis=1, keepdims=True))
                weights = (lifted * (1.0 / jnp.sum(lifted, axis=1, keepdims=True))).astype(BF16)
                mixed = jnp.dot(weights, values, preferred_element_type=F32)
                high = mixed.astype(BF16)
                hi_ref[pl.ds(row, span), h * HEAD_SIZE:(h + 1) * HEAD_SIZE] = high
                lo_ref[pl.ds(row, span), h * HEAD_SIZE:(h + 1) * HEAD_SIZE] = (
                    mixed - high.astype(F32)).astype(BF16)

        below = 0
        for count in widths(spans):
            pl.when((needed > below) & (needed <= count))(functools.partial(attend, count))
            below = count
        return carry

    lax.fori_loop(0, spans, one_span, 0)
    dims = (((0,), (0,)), ((), ()))
    for i in range(TILES):
        hi_l = hi_ref[:, i * TILE:(i + 1) * TILE]
        lo_l = lo_ref[:, i * TILE:(i + 1) * TILE]
        hi_r = hi_ref[:, i * TILE:]
        lo_r = lo_ref[:, i * TILE:]
        gram_ref[0, :, OFFSETS[i]:OFFSETS[i + 1]] = (
            lax.dot_general(hi_l, hi_r, dims, preferred_element_type=F32)
            + lax.dot_general(hi_l, lo_r, dims, preferred_element_type=F32)
            + lax.dot_general(lo_l, hi_r, dims, preferred_element_type=F32))


def attention_grams(query, keys, values, lengths, order, span):
    rows, columns = query.shape
    spans, blocks = rows // span, columns // BLOCK_W
    per_kv = QUERY_HEADS // KEY_VALUE_HEADS * HEAD_SIZE // BLOCK_W
    smem = pl.BlockSpec(memory_space=pltpu.SMEM)
    return pl.pallas_call(
        functools.partial(attention_kernel, span, spans, blocks),
        grid=(blocks,),
        out_shape=jax.ShapeDtypeStruct((blocks, TILE, PACKED), F32),
        in_specs=[
            smem, smem,
            pl.BlockSpec((rows, BLOCK_W), lambda b: (0, b)),
            pl.BlockSpec((rows, HEAD_SIZE), lambda b: (0, b // per_kv)),
            pl.BlockSpec((rows, HEAD_SIZE), lambda b: (0, b // per_kv)),
        ],
        out_specs=pl.BlockSpec((1, TILE, PACKED), lambda b: (b, 0, 0)),
        scratch_shapes=[
            pltpu.VMEM((rows, HEAD_SIZE), BF16),
            pltpu.VMEM((rows, HEAD_SIZE), BF16),
            pltpu.VMEM((rows, BLOCK_W), BF16),
            pltpu.VMEM((rows, BLOCK_W), BF16),
        ],
        name="attention_grams",
    )(lengths, order, query, keys, values)


def split3(x):
    high = x.astype(BF16)
    rest = x - high.astype(F32)
    mid = rest.astype(BF16)
    return high, mid, (rest - mid.astype(F32)).astype(BF16)


def outer6(left, right, axis=0):
    lh, lm, ll = split3(left)
    rh, rm, rl = split3(right)
    lhs = jnp.concatenate([lh, lh, lm, lh, ll, lm], axis=0)
    rhs = jnp.concatenate([rh, rm, rh, rl, rh, rm], axis=0)
    return lax.dot_general(lhs, rhs, (((0,), (0,)), ((), ())), preferred_element_type=F32)


def factor_panel(a_ref, i):
    lo, hi = OFFSETS[i], OFFSETS[i + 1]
    tiles = TILES - i
    sub = lax.broadcasted_iota(jnp.int32, (8, TILE), 0)
    for s in range(TILE // 8):
        rows = slice(8 * s, 8 * s + 8)
        strip = [a_ref[rows, lo + t * TILE:lo + (t + 1) * TILE] for t in range(tiles)]
        cols = [jnp.broadcast_to(strip[0][:, 8 * s + j:8 * s + j + 1], (8, TILE)) for j in range(8)]
        for j in range(8):
            inv = lax.rsqrt(cols[j][j:j + 1, :])
            low = jnp.where(sub > j, cols[j] * inv, 0.0)
            own = sub == j
            for m in range(j + 1, 8):
                cols[m] = cols[m] - low * (cols[m][j:j + 1, :] * inv)
            for t in range(tiles):
                row = strip[t][j:j + 1, :] * inv
                strip[t] = jnp.where(own, row, strip[t] - low * row)
        for t in range(tiles):
            a_ref[rows, lo + t * TILE:lo + (t + 1) * TILE] = strip[t]
        if s < TILE // 8 - 1:
            whole = jnp.concatenate(strip, axis=1)
            update = outer6(strip[0], whole)
            a_ref[8 * s + 8:, lo:hi] = a_ref[8 * s + 8:, lo:hi] - update[8 * s + 8:, :]


def cholesky_kernel(gram_ref, out_ref, a_ref):
    a_ref[...] = gram_ref[0]
    eye = (lax.broadcasted_iota(jnp.int32, (TILE, TILE), 0)
           == lax.broadcasted_iota(jnp.int32, (TILE, TILE), 1))
    trace = jnp.zeros((1, 1), F32)
    for i in range(TILES):
        diag = jnp.where(eye, a_ref[:, OFFSETS[i]:OFFSETS[i] + TILE], 0.0)
        trace = trace + jnp.sum(jnp.sum(diag, axis=1, keepdims=True), axis=0, keepdims=True)
    damp = jnp.where(eye, 0.1 * trace / BLOCK_W, 0.0)
    for i in range(TILES):
        at = slice(OFFSETS[i], OFFSETS[i] + TILE)
        a_ref[:, at] = a_ref[:, at] + damp
    upper = (lax.broadcasted_iota(jnp.int32, (TILE, TILE), 0)
             <= lax.broadcasted_iota(jnp.int32, (TILE, TILE), 1))
    for i in range(TILES):
        factor_panel(a_ref, i)
        at = slice(OFFSETS[i], OFFSETS[i] + TILE)
        for t in range(i + 1, TILES):
            left = a_ref[:, OFFSETS[i] + (t - i) * TILE:OFFSETS[i] + (t - i + 1) * TILE]
            right = a_ref[:, OFFSETS[i] + (t - i) * TILE:OFFSETS[i + 1]]
            a_ref[:, OFFSETS[t]:OFFSETS[t + 1]] = (
                a_ref[:, OFFSETS[t]:OFFSETS[t + 1]] - outer6(left, right))
        a_ref[:, at] = jnp.where(upper, a_ref[:, at], 0.0)
    out_ref[0] = a_ref[...]


def factor(grams):
    spec = pl.BlockSpec((1, TILE, PACKED), lambda b: (b, 0, 0))
    return pl.pallas_call(
        cholesky_kernel,
        grid=(grams.shape[0],),
        out_shape=jax.ShapeDtypeStruct(grams.shape, F32),
        in_specs=[spec],
        out_specs=spec,
        scratch_shapes=[pltpu.VMEM((TILE, PACKED), F32)],
        name="factor",
    )(grams)


def whiten_kernel(u_ref, w_ref, out_ref):
    for i in range(TILES):
        upper = u_ref[0, :, OFFSETS[i]:OFFSETS[i + 1]]
        high = upper.astype(BF16)
        low = (upper - high.astype(F32)).astype(BF16)
        weight = w_ref[:, i * TILE:]
        both = lax.dot_general(jnp.concatenate([high, low], axis=0), weight,
                               (((1,), (1,)), ((), ())), preferred_element_type=F32)
        out_ref[0, i * TILE:(i + 1) * TILE, :] = both[:TILE] + both[TILE:]


def whiten(upper, weight):
    blocks, outs = upper.shape[0], weight.shape[0]
    step = min(outs, 1024)
    return pl.pallas_call(
        whiten_kernel,
        grid=(blocks, outs // step),
        out_shape=jax.ShapeDtypeStruct((blocks, BLOCK_W, outs), F32),
        in_specs=[
            pl.BlockSpec((1, TILE, PACKED), lambda b, o: (b, 0, 0)),
            pl.BlockSpec((step, BLOCK_W), lambda b, o: (o, b)),
        ],
        out_specs=pl.BlockSpec((1, BLOCK_W, step), lambda b, o: (b, 0, o)),
        name="whiten",
    )(upper, weight)


def by_heads(rows, count):
    return lax.all_to_all(rows, "seq", split_axis=1, concat_axis=0, tiled=True)


def shards(query_rows, key_rows, placed_value_rows, doc_lengths, span_order, out_weight):
    tok_count = query_rows.shape[1]
    seq_count = lax.axis_size("seq")
    dp_count = lax.axis_size("dp")
    span = tok_count * seq_count // span_order.shape[1]
    query = by_heads(query_rows[0], seq_count)
    keys = by_heads(key_rows[0], seq_count)
    values = by_heads(placed_value_rows[0], seq_count)
    grams = attention_grams(query, keys, values, doc_lengths, span_order, span)
    if grams.shape[0] % dp_count == 0:
        own = lax.psum_scatter(grams, "dp", scatter_dimension=0, tiled=True)
        upper = lax.all_gather(factor(own), "dp", axis=0, tiled=True)
    else:
        upper = factor(lax.psum(grams, "dp"))
    return whiten(upper, out_weight)


def solution(mesh):
    in_specs = (
        P(("groups", "dp"), "seq", None),
        P(("groups", "dp"), "seq", None),
        P(("groups", "dp"), "seq", None),
        P(("groups", "dp"), None),
        P(("groups", "dp"), None),
        P("dp", "seq"),
    )
    out_specs = P(("groups", "seq"), None, "dp")
    return jax.shard_map(shards, mesh=mesh, in_specs=in_specs, out_specs=out_specs, check_vma=False)
```

time: 881 us -> 299 us (0.34); the launches traced: 871 us -> 298 us
  other arithmetic: 326 us -> 0 us
  waiting for transfers between devices: 304 us -> 114 us
  matrix products: 178 us -> 0 us
  Pallas kernels: 0 us -> 89.9 us
  blocking collectives: 0 us -> 54 us
  local copies, waits for them, and re-layouts: 48.8 us -> 18.9 us
    another operation x17 -> x0, other arithmetic: 308 us -> none  [the longest x16 307 us: shards(): upper = jnp.swapaxes(jnp.linalg.cholesky(summed), 1, 2)]
    psum x1 -> x0, waiting for transfers between devices: 155 us -> none  [shards(): summed = lax.psum(damped, 'dp')]
    dot_general x10 -> x0, matrix products: 94.9 us -> none  [the longest x8 38.6 us: local_attention(): jnp.einsum('gqk,kd->qgd', weights, value_head, preferred_element_type=jnp...]
    pallas_call x0 -> x3, Pallas kernels: none -> 89.9 us  [the longest x1 49.8 us: attention_grams(): pl.pallas_call(functools.partial(attention_kernel, span, spans, blocks),...]
    reduce_scatter x1, waiting for transfers between devices: 125 us -> 52.7 us  [shards(): own = lax.psum_scatter(grams, 'dp', scatter_dimension=0, tiled=True)]
    sub x8 -> x0, matrix products: 71.5 us -> none  [local_attention(): lifted = jnp.exp(scores - largest)]
    all_to_all x0 -> x1, blocking collectives: none -> 54 us  [by_heads(): return lax.all_to_all(rows, 'seq', split_axis=1, concat_axis=0, tiled=True)]
    all_gather x2 -> x1, waiting for transfers between devices: 22.9 us -> 54.4 us  [shards(): upper = lax.all_gather(factor(own), 'dp', axis=0, tiled=True)]
  transfers between devices with their start and end apart: 4 -> 4, of which waited for: 4 -> 3; matrix products, arithmetic and copies ran while one was open for 3% -> 2% of each run, Pallas kernels for 0% -> 0%
where the time goes in v1:
time: 299 us; the launch traced here: 298 us
  waiting for transfers between devices  114 us (38%)
  Pallas kernels  89.9 us (30%)
  blocking collectives  54 us (18%)
  local copies, waits for them, and re-layouts  18.9 us (6%)
  between operations  13.4 us (4%)
  starting transfers between devices  8.01 us (3%)
    all_gather x1, waiting for transfers between devices, shards(): upper = lax.all_gather(factor(own), 'dp', axis=0, tiled=True)  54.4 us
    all_to_all x1, blocking collectives, by_heads(): return lax.all_to_all(rows, 'seq', split_axis=1, concat_axis=0, tiled=True)  54 us
    reduce_scatter x1, waiting for transfers between devices, shards(): own = lax.psum_scatter(grams, 'dp', scatter_dimension=0, tiled=True)  52.7 us
    pallas_call x1, Pallas kernels, attention_grams(): pl.pallas_call(functools.partial(attention_kernel, span, spans, blocks),...  49.8 us
    pallas_call x1, Pallas kernels, factor(): pl.pallas_call(cholesky_kernel, grid=(grams.shape[0],), out_shape=jax.Sha...  24.1 us
    all_to_all x6, local copies, waits for them, and re-layouts, by_heads(): return lax.all_to_all(rows, 'seq', split_axis=1, concat_axis=0, tiled=True)  18.9 us
    pallas_call x1, Pallas kernels, whiten(): pl.pallas_call(whiten_kernel, grid=(blocks, outs // step), out_shape=jax....  16 us
    all_to_all x2, starting transfers between devices, by_heads(): return lax.all_to_all(rows, 'seq', split_axis=1, concat_axis=0, tiled=True)  7.71 us
  transfers between devices with their start and end apart: 4, of which 3 were waited for; matrix products, arithmetic and copies ran while one was open for 2% of the time, Pallas kernels for 0%

profile of v1, /device:TPU:0, one launch (start us, length us, event | category | flops | bytes accessed | tf_op | source)
XLA Modules:
  0.0 297.9 jit_solution(13058576636663975979)
XLA Ops:
  6.5 1.4 all_to_all.46
  8.0 0.9 copy.11
  8.8 4.2 %all-to-all-start.1 = ((bf16[256,4,256]{2,0,1:T(8,128)(2,1)}), bf16[256,4,256]{2,0,1:T(8,128)(2,1)S(1)}, u32[]{:S(2)}, u32[]{:S(2)}) async-start(bf16[256,4,256]{2,0,1:T(8,128)(2,1)} %copy.11), calls=%async_computation.1 | async-start | bytes 1048576 | tf_op jit(solution)/shard_map/all_to_all | solution.py:231
  13.1 1.4 all_to_all.50
  14.5 0.9 copy.12
  15.4 6.5 %all-to-all-done.1 = bf16[256,4,256]{2,0,1:T(8,128)(2,1)S(1)} async-done(((bf16[256,4,256]{2,0,1:T(8,128)(2,1)}), bf16[256,4,256]{2,0,1:T(8,128)(2,1)S(1)}, u32[]{:S(2)}, u32[]{:S(2)}) %all-to-all-start.1) | async-done | bytes 524320 | tf_op jit(solution)/shard_map/all_to_all | solution.py:231
  21.9 0.0 copy-start
  21.9 3.5 %all-to-all-start.2 = ((bf16[256,4,256]{2,0,1:T(8,128)(2,1)}), bf16[256,4,256]{2,0,1:T(8,128)(2,1)S(1)}, u32[]{:S(2)}, u32[]{:S(2)}) async-start(bf16[256,4,256]{2,0,1:T(8,128)(2,1)} %copy.12), calls=%async_computation.2 | async-start | bytes 1048576 | tf_op jit(solution)/shard_map/all_to_all | solution.py:231
  25.4 0.0 reduce-scatter.2.cloned.1.call-start
  25.4 7.8 %all_to_all.42 = bf16[256,4,2048]{2,1,0:T(4,128)(2,1)} reshape(bf16[1,256,8192]{2,1,0:T(8,128)(2,1)} %param.6) | data formatting | bytes 8388608 | tf_op jit(solution)/shard_map/all_to_all | solution.py:231
  33.2 0.0 copy-done
  33.2 6.4 %copy.10 = bf16[256,4,2048]{2,0,1:T(8,128)(2,1)} copy(bf16[256,4,2048]{2,1,0:T(4,128)(2,1)} %all_to_all.42) | data formatting | bytes 8388608 | tf_op jit(solution)/shard_map/all_to_all | solution.py:231
  39.7 0.0 all-to-all-done.2
  39.7 0.0 copy-start.1
  39.7 54.0 %all_to_all.57 = bf16[256,4,2048]{2,0,1:T(8,128)(2,1)} all-to-all(bf16[256,4,2048]{2,0,1:T(8,128)(2,1)} %copy.10), channel_id=1, replica_groups=mesh['groups'=2,'dp'=4,'seq'=4] {'seq'}, dimensions={1} | all-to-all | bytes 8388608 | tf_op jit(solution)/shard_map/all_to_all | solution.py:231
  93.6 0.0 copy-done.1
  93.6 49.8 %attention_grams.1 = f32[4,128,1280]{2,1,0:T(8,128)} custom-call(s32[1,8]{1,0:T(1,128)} %lengths_ref.1, s32[1,8]{1,0:T(1,128)} %order_ref.1, bf16[1024,2048]{1,0:T(8,128)(2,1)} %bitcast.9, bf16[1024,256]{1,0:T(8,128)(2,1)} %bitcast.10, bf16[1024,256]{1,0:T(8,128)(2,1)} %bitcast.11), custom_call_target="tpu_custom_call" | custom-call | tf_op jit(solution)/shard_map/attention_grams/pallas_call | solution.py:103
  143.5 0.0 reduce-scatter.2.cloned.1.call-update
  143.5 0.3 all-gather.2.cloned.1.call-start
  143.7 52.7 %reduce-scatter.2.cloned.1.call-done.gram_ref = f32[1,128,1280]{2,1,0:T(8,128)} async-done(((f32[4,128,1280]{2,1,0:T(8,128)}), f32[1,128,1280]{2,1,0:T(8,128)}) %reduce-scatter.2.cloned.1.call-update) | async-done | bytes 655376 | tf_op jit(solution)/shard_map/reduce_scatter | solution.py:244
  196.4 24.1 %factor.1 = f32[1,128,1280]{2,1,0:T(8,128)} custom-call(f32[1,128,1280]{2,1,0:T(8,128)} %reduce-scatter.2.cloned.1.call-done.gram_ref), custom_call_target="tpu_custom_call" | custom-call | tf_op jit(solution)/shard_map/factor/pallas_call | solution.py:192
  220.5 0.0 all-gather.2.cloned.1.call-update
  220.6 54.4 %all-gather.2.cloned.1.call-done.u_ref = f32[4,128,1280]{2,1,0:T(8,128)} async-done(((f32[1,128,1280]{2,1,0:T(8,128)}), f32[4,128,1280]{2,1,0:T(8,128)}) %all-gather.2.cloned.1.call-update) | async-done | bytes 2621456 | tf_op jit(solution)/shard_map/all_gather | solution.py:245
  275.0 16.0 %whiten.1 = f32[4,512,2048]{2,1,0:T(8,128)} custom-call(f32[4,128,1280]{2,1,0:T(8,128)} %all-gather.2.cloned.1.call-done.u_ref, bf16[2048,2048]{1,0:T(8,128)(2,1)} %w_ref.1), custom_call_target="tpu_custom_call" | custom-call | tf_op jit(solution)/shard_map/whiten/pallas_call | solution.py:217
Async XLA Ops:
  8.8 13.1 %all-to-all-start.1 = ((bf16[256,4,256]{2,0,1:T(8,128)(2,1)}), bf16[256,4,256]{2,0,1:T(8,128)(2,1)S(1)}, u32[]{:S(2)}, u32[]{:S(2)}) async-start(bf16[256,4,256]{2,0,1:T(8,128)(2,1)} %copy.11), calls=%async_computation.1 | async-start | bytes 1048576 | tf_op jit(solution)/shard_map/all_to_all | solution.py:231
  21.9 11.3 %copy-start = (bf16[256,4,256]{2,0,1:T(8,128)(2,1)}, bf16[256,4,256]{2,0,1:T(8,128)(2,1)S(1)}, u32[]{:S(2)}) copy-start(bf16[256,4,256]{2,0,1:T(8,128)(2,1)S(1)} %all-to-all-done.1) | copy-start | bytes 1572868
  21.9 17.8 %all-to-all-start.2 = ((bf16[256,4,256]{2,0,1:T(8,128)(2,1)}), bf16[256,4,256]{2,0,1:T(8,128)(2,1)S(1)}, u32[]{:S(2)}, u32[]{:S(2)}) async-start(bf16[256,4,256]{2,0,1:T(8,128)(2,1)} %copy.12), calls=%async_computation.2 | async-start | bytes 1048576 | tf_op jit(solution)/shard_map/all_to_all | solution.py:231
  25.4 171.1 %reduce-scatter.2.cloned.1.call-start = ((), (), s32[]{:S(2)}) async-start(), calls=%async_computation.4 | async-start | bytes 3276800 | tf_op jit(solution)/shard_map/reduce_scatter | solution.py:244
  39.7 54.0 %copy-start.1 = (bf16[256,4,256]{2,0,1:T(8,128)(2,1)}, bf16[256,4,256]{2,0,1:T(8,128)(2,1)S(1)}, u32[]{:S(2)}) copy-start(bf16[256,4,256]{2,0,1:T(8,128)(2,1)S(1)} %all-to-all-done.2) | copy-start | bytes 1572868
  143.5 131.5 %all-gather.2.cloned.1.call-start = ((), (), s32[]{:S(2)}) async-start(), calls=%async_computation.5 | async-start | bytes 3276800 | tf_op jit(solution)/shard_map/all_gather | solution.py:245
Sparse Core Ops, SparseCore 0:
  143.6 52.8 reduce-scatter.1
  220.7 54.2 all-gather.1
